TPU v7x, 32 devices: a whole 2x2x4 slice. The times are simulated.
32 devices in a mesh: groups: 2 (over y), dp: 2 (over x), ctx: 4 (over z), tp: 2 (over core).
Axes of the slice: x: 2, y: 2, z: 4, core: 2. Of those that a mesh axis runs over, the one named last changes fastest.
Arguments:
- queries: bfloat16 [4, 1024, 2048], P(('groups', 'dp'), 'ctx', 'tp'), parts along dimension 0, may hold values from -20 to 20
- keyvals: bfloat16 [4, 1024, 2, 512], P(('groups', 'dp'), 'ctx', None, 'tp'), parts along dimension 0, may hold values from -20 to 20
- doc_ids: int32 [4, 1024], P(('groups', 'dp'), 'ctx'), parts along dimension 0, may hold values from 0 to 64, as said below
- plan: int32 [4, 4], P(('groups', 'dp')), parts along dimension 0, may hold values from 0 to 3, as said below
- lengths: int32 [4, 8], P(('groups', 'dp')), parts along dimension 0, may hold values from 1 to 512, 1024 in all within a row
- out_weight: bfloat16 [2048, 4096], P('tp', 'dp'), may hold values from -0.5 to 0.5
Outputs:
- mixed_out: bfloat16 [4, 1024, 4096], P(('groups', 'dp'), 'ctx', 'tp'), parts along dimension 0
There are 2 independent parts, one for each index of `groups`. A program takes and returns all parts, laid end to end along the dimension named above; an argument that names none is the same for every part. Nothing has to cross between parts.
Inputs may be any that keep to these rules, and one draw needn't show every extreme that they name: `lengths`: each row sums to 1024. `plan`: each row names every block of its request group once. `doc_ids`: 0 marks tokens that see every earlier token of their request.
All inputs are finite; a program needn't handle non-finite values.
Results may differ from a plain program's by a relative error of at most 0.0061.
Values may be sent and summed in bfloat16 or wider, within the bound.
A program may use at most 128 MiB of HBM per device.

v0:
```python
import jax
import jax.numpy as jnp
from jax import lax
from jax.sharding import PartitionSpec as P

HD = 128


def request_of(positions, request_ends):
    return jnp.sum((request_ends[None, :] <= positions[:, None]).astype(jnp.int32), axis=1)


def per_device(queries, keyvals, doc_ids, plan, lengths, out_weight):
    tok_count = queries.shape[1]
    kv_width = keyvals.shape[3]
    kv_local = kv_width // HD
    heads_local = queries.shape[2] // HD
    group_size = heads_local // kv_local
    cycle_size = lax.axis_size("ctx")
    slot_index = lax.axis_index("ctx")
    placing = plan[0]
    request_ends = jnp.cumsum(lengths[0])
    offsets = jnp.arange(tok_count, dtype=jnp.int32)
    query_pos = placing[slot_index] * tok_count + offsets
    query_req = request_of(query_pos, request_ends)
    query_doc = doc_ids[0]
    query_heads = queries[0].reshape(tok_count, kv_local, group_size, HD)
    inv_root = HD ** (-0.5)

    def key_block(running, kv_block, doc_block, key_pos):
        key_req = request_of(key_pos, request_ends)
        allowed = (query_req[:, None] == key_req[None, :]) & (
            key_pos[None, :] <= query_pos[:, None]
        )
        allowed = allowed & ((query_doc[:, None] == doc_block[None, :]) | (query_doc[:, None] == 0))

        def attend(state):
            row_max, row_sum, weighted = state
            key_heads = kv_block[:, 0].reshape(-1, kv_local, HD)
            value_heads = kv_block[:, 1].reshape(-1, kv_local, HD)
            scores = (
                jnp.einsum(
                    "tkgd,nkd->kgtn", query_heads, key_heads, preferred_element_type=jnp.float32
                )
                * inv_root
            )
            scores = jnp.where(allowed, scores, -1e30)
            new_max = jnp.maximum(row_max, jnp.max(scores, axis=3))
            probs = jnp.where(allowed, jnp.exp(scores - new_max[..., None]), 0.0)
            factor = jnp.exp(row_max - new_max)
            new_sum = row_sum * factor + jnp.sum(probs, axis=3)
            update = jnp.einsum(
                "kgtn,nkd->kgtd",
                probs.astype(jnp.bfloat16),
                value_heads,
                preferred_element_type=jnp.float32,
            )
            return (new_max, new_sum, weighted * factor[..., None] + update)

        return lax.cond(jnp.any(allowed), attend, lambda state: state, running)

    start_state = (
        jnp.full((kv_local, group_size, tok_count), -1e30, jnp.float32),
        jnp.zeros((kv_local, group_size, tok_count), jnp.float32),
        jnp.zeros((kv_local, group_size, tok_count, HD), jnp.float32),
    )
    running = start_state
    kv_piece = lax.all_gather(keyvals[0], "ctx", axis=0, tiled=True)
    doc_piece = lax.all_gather(query_doc, "ctx", axis=0, tiled=True)
    piece_rows = kv_piece.shape[0]
    row_ids = jnp.arange(piece_rows, dtype=jnp.int32)
    owner = row_ids // tok_count
    matches = owner[:, None] == jnp.arange(cycle_size, dtype=jnp.int32)[None, :]
    block_ids = jnp.sum(jnp.where(matches, placing[None, :], 0), axis=1)
    key_pos = block_ids * tok_count + row_ids % tok_count
    width = 512
    count = piece_rows // width

    def step(state, block):
        return (key_block(state, block[0], block[1], block[2]), None)

    stacked = (
        kv_piece.reshape(count, width, 2, kv_width),
        doc_piece.reshape(count, width),
        key_pos.reshape(count, width),
    )
    running, unused = lax.scan(step, running, stacked)
    row_max, row_sum, weighted = running
    attended = (
        (weighted / row_sum[..., None])
        .transpose(2, 0, 1, 3)
        .reshape(tok_count, heads_local * HD)
        .astype(jnp.bfloat16)
    )
    projected = jnp.dot(
        lax.all_gather(attended, "dp", axis=0, tiled=True),
        out_weight,
        preferred_element_type=jnp.float32,
    ).astype(jnp.bfloat16)
    column_set = lax.all_to_all(projected, "dp", split_axis=0, concat_axis=1, tiled=True)
    partials = column_set.astype(jnp.float32)
    mixed_out = lax.psum_scatter(
        partials.astype(jnp.bfloat16), "tp", scatter_dimension=1, tiled=True
    )
    return mixed_out[None]


def solution(mesh):
    placed = (
        P(("groups", "dp"), "ctx", "tp"),
        P(("groups", "dp"), "ctx", None, "tp"),
        P(("groups", "dp"), "ctx"),
        P(("groups", "dp"), None),
        P(("groups", "dp"), None),
        P("tp", "dp"),
    )
    return jax.shard_map(
        per_device,
        mesh=mesh,
        in_specs=placed,
        out_specs=P(("groups", "dp"), "ctx", "tp"),
        check_vma=False,
    )
```

profile of v0, /device:TPU:1, one launch (start us, length us, event | category | flops | bytes accessed | tf_op | source)
XLA Modules:
  0.0 124.9 jit_solution(14108327814357423036)
XLA Ops:
  6.5 1.7 %copy.28 = bf16[1,256,2,256]{3,1,2,0:T(8,128)(2,1)} copy(bf16[1,256,2,256]{3,2,1,0:T(2,128)(2,1)} %param.11) | data formatting | bytes 524288 | tf_op args[1]
  8.3 0.8 reduce-window.8
  9.1 10.2 %all-gather = s32[1,1024]{1,0:T(1,128)S(1)} all-gather(s32[1,256]{1,0:T(1,128)} %param.12), channel_id=2, replica_groups=mesh['groups'=2,'dp'=2,'ctx'=4,'tp'=2] {'ctx'}, dimensions={1}, use_global_device_ids=true | all-gather | bytes 5120 | tf_op jit(solution)/shard_map/all_gather | solution.py:69
  19.3 0.6 broadcast.82
  19.9 0.7 reduce.3
  20.7 1.2 copy.29
  21.9 0.3 copy.31
  22.2 1.3 %fusion.21 = s32[1,1]{1,0:T(1,128)} fusion(s32[1,4]{1,0:T(1,128)} %param.13, s32[]{:T(128)S(6)} %select_n.33), kind=kLoop, calls=%fused_computation.43 | loop fusion | flops 1 | bytes 12 | tf_op jit(solution)/shard_map/mul | solution.py:24
  23.5 0.7 select_reduce_fusion
  24.3 0.7 iota_add_fusion.1
  25.1 13.4 %all-gather.7.cloned.1.call-done = bf16[1,1024,2,256]{3,1,2,0:T(8,128)(2,1)} async-done(((bf16[1,256,2,256]{3,1,2,0:T(8,128)(2,1)}), bf16[1,1024,2,256]{3,1,2,0:T(8,128)(2,1)}) %all-gather.7.cloned.1.call-update) | async-done | bytes 1048592 | tf_op jit(solution)/shard_map/all_gather | solution.py:68
  38.5 1.5 %copy.30 = bf16[2,512,2,256]{1,3,2,0:T(8,128)(2,1)S(1)} copy(bf16[2,512,2,256]{3,1,0,2:T(8,128)(2,1)} %bitcast.67) | data formatting | bytes 2097152
  40.1 12.4 %while.15 = (s32[]{:T(128)}, f32[2,4,256]{2,1,0:T(4,128)S(1)}, f32[2,4,256]{2,1,0:T(4,128)S(1)}, f32[2,4,256,128]{3,2,1,0:T(8,128)S(1)}, s32[256]{0:T(256)S(1)},...) while((s32[]{:T(128)}, f32[2,4,256]{2,1,0:T(4,128)S(1)}, ...), condition=%wide.region_10.11_spmd.clone, body=%wide.region_3.10_spmd.clone.sunk | while | flops 551960576 | bytes 18505504 | solution.py:87
  40.2 0.7 iota_add_fusion.3
  40.9 0.9 fusion.28
  42.5 3.8 %conditional.3 = ((f32[2,4,256]{2,1,0:T(4,128)S(1)}, f32[2,4,256]{2,1,0:T(4,128)S(1)}, f32[2,4,256,128]{3,2,1,0:T(8,128)S(1)})) conditional(s32[]{:T(128)} %convert_element_type.45, (f32[2,4,256]{2,1,0:T(4,128)S(1)}, f32[2,4,256]{2,1,0:T(4,128)S(1)}, f32[2,4,256,128]{3,2,1,0:T(8,128)S(1)}) %tuple.47, (pred[256,512]{0,1:T(8,128)(4,1)S(1)}, ...), branch_computations={%region_6.6_spmd, %region_7.9_spmd} | conditional | flops 551030784 | bytes 18350116 | solution.py:60
  42.6 0.9 fusion.2
  43.5 1.0 fusion.4
  44.6 1.8 %fusion.8 = f32[2,4,256,128]{3,2,1,0:T(8,128)S(1)} fusion(bf16[512,2,128,1]{0,2,3,1:T(8,128)(2,1)S(1)} %bitcast.62, f32[2,512,256,4]{2,1,3,0:T(8,128)S(1)} %get-tuple-element.214, f32[2,4,256]{2,1,0:T(4,128)S(1)} %max.3, pred[256,512]{0,1:T(8,128)(4,1)S(1)} %get-tuple-element.91, f32[2,4,256,128]{3,2,1,0:T(8,128)S(1)} %get-tuple-element.96, ...), kind=kOutput, calls=%fused_computation.8 | convolution fusion | flops 274202624 | bytes 6701056 | tf_op jit(solution)/shard_map/while/body/eval_jaxpr/cond/branch_1_fun/kgtn,nkd->kgtd/dot_general | solution.py:52
  46.5 0.7 iota_add_fusion.3
  47.2 0.9 fusion.28
  48.7 3.8 %conditional.3 = ((f32[2,4,256]{2,1,0:T(4,128)S(1)}, f32[2,4,256]{2,1,0:T(4,128)S(1)}, f32[2,4,256,128]{3,2,1,0:T(8,128)S(1)})) conditional(s32[]{:T(128)} %convert_element_type.45, (f32[2,4,256]{2,1,0:T(4,128)S(1)}, f32[2,4,256]{2,1,0:T(4,128)S(1)}, f32[2,4,256,128]{3,2,1,0:T(8,128)S(1)}) %tuple.47, (pred[256,512]{0,1:T(8,128)(4,1)S(1)}, ...), branch_computations={%region_6.6_spmd, %region_7.9_spmd} | conditional | flops 551030784 | bytes 18350116 | solution.py:60
  48.8 0.9 fusion.2
  49.8 1.0 fusion.4
  50.8 1.8 %fusion.8 = f32[2,4,256,128]{3,2,1,0:T(8,128)S(1)} fusion(bf16[512,2,128,1]{0,2,3,1:T(8,128)(2,1)S(1)} %bitcast.62, f32[2,512,256,4]{2,1,3,0:T(8,128)S(1)} %get-tuple-element.214, f32[2,4,256]{2,1,0:T(4,128)S(1)} %max.3, pred[256,512]{0,1:T(8,128)(4,1)S(1)} %get-tuple-element.91, f32[2,4,256,128]{3,2,1,0:T(8,128)S(1)} %get-tuple-element.96, ...), kind=kOutput, calls=%fused_computation.8 | convolution fusion | flops 274202624 | bytes 6701056 | tf_op jit(solution)/shard_map/while/body/eval_jaxpr/cond/branch_1_fun/kgtn,nkd->kgtd/dot_general | solution.py:52
  52.6 0.3 copy.32
  52.9 0.9 divide_convert_fusion
  53.9 20.1 %all-gather.5.cloned.1.call-done = bf16[512,1024]{0,1:T(8,128)(2,1)} async-done(((bf16[256,1024]{0,1:T(8,128)(2,1)}), bf16[512,1024]{0,1:T(8,128)(2,1)}) %all-gather.5.cloned.1.call-update) | async-done | bytes 1048592 | tf_op jit(solution)/shard_map/all_gather | solution.py:96
  74.0 4.9 %convolution_convert_fusion = bf16[512,2048]{1,0:T(8,128)(2,1)S(1)} fusion(bf16[512,1024]{0,1:T(8,128)(2,1)} %all-gather.5.cloned.1.call-done, bf16[1024,2048]{1,0:T(8,128)(2,1)} %param.15), kind=kOutput, calls=%fused_computation.21 | convolution fusion | flops 2148532224 | bytes 7340032 | tf_op jit(solution)/shard_map/dot_general | solution.py:95
  78.9 26.6 %all_to_all.19 = bf16[2,256,2048]{2,1,0:T(8,128)(2,1)S(1)} all-to-all(bf16[2,256,2048]{2,1,0:T(8,128)(2,1)S(1)} %bitcast.65), channel_id=1, replica_groups=mesh['groups'=2,'dp'=2,'ctx'=4,'tp'=2] {'dp'}, dimensions={0} | all-to-all | bytes 4194304 | tf_op jit(solution)/shard_map/all_to_all | solution.py:100
  105.5 1.5 %copy.41 = bf16[2,32,8,2048]{3,2,0,1:T(8,128)(2,1)} copy(bf16[2,32,8,2048]{3,2,1,0:T(8,128)(2,1)S(1)} %bitcast.61) | data formatting | bytes 4194304 | tf_op jit(solution)/shard_map/all_to_all | solution.py:100
  107.0 11.3 %reduce-scatter.2.cloned.1.call-done = bf16[256,2048]{1,0:T(8,128)(2,1)} async-done(((bf16[256,4096]{1,0:T(8,128)(2,1)}), bf16[256,2048]{1,0:T(8,128)(2,1)}) %reduce-scatter.2.cloned.1.call-update) | async-done | bytes 1048592 | tf_op jit(solution)/shard_map/reduce_scatter | solution.py:102
  (33 shorter events, 0.7 us)
Async XLA Ops:
  6.5 33.6 %copy-start = (s32[1,256]{1,0:T(1,128)S(1)}, s32[1,256]{1,0:T(1,128)}, u32[]{:S(2)}) copy-start(s32[1,256]{1,0:T(1,128)} %param.12) | copy-start | bytes 3076
  6.5 32.0 %all-gather.7.cloned.1.call-start = ((), (), s32[]{:S(2)}) async-start(), calls=%async_computation.4 | async-start | bytes 1310720 | tf_op jit(solution)/shard_map/all_gather | solution.py:68
  8.3 65.8 %all-gather.5.cloned.1.call-start = ((), (), s32[]{:S(2)}) async-start(), calls=%async_computation.2 | async-start | bytes 1572864 | tf_op jit(solution)/shard_map/all_gather | solution.py:96
  53.8 64.5 %reduce-scatter.2.cloned.1.call-start = ((), (), s32[]{:S(2)}) async-start(), calls=%async_computation.3 | async-start | bytes 3145728 | tf_op jit(solution)/shard_map/reduce_scatter | solution.py:102
Sparse Core Ops, SparseCore 0:
  8.9 29.5 all-gather.6
  54.0 20.0 all-gather.4
  107.2 11.1 reduce-scatter.1
where the time goes:
time: 126 us; the launch traced here: 125 us
  waiting for transfers between devices  44.9 us (36%)
  blocking collectives  36.8 us (29%)
  between operations  13.2 us (10%)
  other arithmetic  10.7 us (8%)
  matrix products  10.2 us (8%)
  local copies, waits for them, and re-layouts  7.4 us (6%)
  loops' own time  1.51 us (1%)
    all_to_all x1, blocking collectives, per_device(): lax.all_to_all(projected, 'dp', split_axis=0, concat_axis=1, tiled=True)  26.6 us
    all_gather x1, waiting for transfers between devices, per_device(): lax.all_gather(attended, 'dp', axis=0, tiled=True)  20.1 us
    all_gather x1, waiting for transfers between devices, per_device(): kv_piece = lax.all_gather(keyvals[0], 'ctx', axis=0, tiled=True)  13.4 us
    reduce_scatter x1, waiting for transfers between devices, per_device(): lax.psum_scatter(partials.astype(jnp.bfloat16), 'tp', scatter_dimension=1...  11.3 us
    all_gather x1, blocking collectives, per_device(): doc_piece = lax.all_gather(query_doc, 'ctx', axis=0, tiled=True)  10.2 us
    dot_general x1, matrix products, per_device(): jnp.dot(lax.all_gather(attended, 'dp', axis=0, tiled=True), out_weight, p...  4.88 us
    unnamed x6, local copies, waits for them, and re-layouts  4.71 us
    dot_general x2, matrix products, attend(): jnp.einsum('kgtn,nkd->kgtd', probs.astype(jnp.bfloat16), value_heads, pre...  3.51 us
  transfers between devices with their start and end apart: 3, of which 3 were waited for; matrix products, arithmetic and copies ran while one was open for 5% of the time, Pallas kernels for 0%

commit v1 on v0

v1 whole, which is shorter than its diff:
```python
import functools
import math

import jax
import jax.numpy as jnp
from jax import lax
from jax.experimental import pallas as pl
from jax.experimental.pallas import tpu as pltpu
from jax.sharding import PartitionSpec as P

HD = 128
LANES = 128
MESH = pl.DeviceIdType.MESH
NEG = -1e30


def wide(x, width):
    return jnp.concatenate([x] * (width // LANES), axis=1) if width > LANES else x


def kernel(
    cfg,
    plan_ref,
    len_ref,
    q_ref,
    kv_ref,
    doc_ref,
    w_hbm,
    out_hbm,
    kvbuf,
    dbuf,
    lo_buf,
    qd_buf,
    m_buf,
    l_buf,
    acc_buf,
    att,
    w_buf,
    part,
    prec,
    fin,
    w_sem,
    kv_send,
    kv_recv,
    doc_send,
    doc_recv,
    att_send,
    att_recv,
    part_send,
    part_recv,
    fin_send,
    fin_recv,
    loc_sem,
):
    n, rows, cores, tok, kvh, gsz, reqs, cols, halves, chunks = cfg
    me = lax.axis_index("ctx")
    d = lax.axis_index("dp")
    t = lax.axis_index("tp")
    other = 1 - t
    hrows = tok // halves
    ccols = cols // chunks
    gcols = gsz * HD
    per_half = rows // cores
    scale = HD ** (-0.5) * math.log2(math.e)

    w_copy = pltpu.make_async_copy(w_hbm, w_buf, w_sem)
    w_copy.start()

    barrier = pltpu.get_barrier_semaphore()

    @pl.when(me > 0)
    def _():
        pl.semaphore_signal(barrier, inc=1, device_id={"ctx": me - 1}, device_id_type=MESH)

    @pl.when(me < n - 1)
    def _():
        pl.semaphore_signal(barrier, inc=1, device_id={"ctx": me + 1}, device_id_type=MESH)

    for k in range(rows):
        for c in range(cores):
            if k == 0 and c == 0:
                continue
            pl.semaphore_signal(
                barrier,
                inc=1,
                device_id={"dp": lax.rem(d + k, rows), "tp": lax.rem(t + c, cores)},
                device_id_type=MESH,
            )
    ends = (me > 0).astype(jnp.int32) + (me < n - 1).astype(jnp.int32)
    pl.semaphore_wait(barrier, rows * cores - 1 + ends)

    def kv_copy(way, step, g, src, block):
        return pltpu.make_async_remote_copy(
            src_ref=src,
            dst_ref=kvbuf.at[block, g],
            send_sem=kv_send.at[way, step, g],
            recv_sem=kv_recv.at[way, step, g],
            device_id={"ctx": me + 1 if way == 0 else me - 1},
            device_id_type=MESH,
        )

    def doc_copy(way, step, src, block):
        return pltpu.make_async_remote_copy(
            src_ref=src,
            dst_ref=dbuf.at[block],
            send_sem=doc_send.at[way, step],
            recv_sem=doc_recv.at[way, step],
            device_id={"ctx": me + 1 if way == 0 else me - 1},
            device_id_type=MESH,
        )

    can = (me < n - 1, me > 0)
    for way in range(2):

        @pl.when(can[way])
        def _(way=way):
            doc_copy(way, 0, doc_ref, me).start()
            for g in range(kvh):
                kv_copy(way, 0, g, kv_ref.at[g], me).start()

    qpos = plan_ref[0, me] * tok + lax.broadcasted_iota(jnp.int32, (tok, LANES), 0)
    low = jnp.zeros((tok, LANES), jnp.int32)
    start = jnp.int32(0)
    for i in range(reqs):
        low = jnp.where(start <= qpos, start, low)
        start = start + len_ref[0, i]
    lo_buf[...] = low
    qd_buf[...] = jnp.transpose(
        jnp.broadcast_to(doc_ref[...].astype(jnp.float32), (LANES, tok))
    )

    def attend(g, kref, dref, block, first):
        row = lax.broadcasted_iota(jnp.int32, (tok, tok), 0)
        col = lax.broadcasted_iota(jnp.int32, (tok, tok), 1)
        q_pos = plan_ref[0, me] * tok + row
        k_pos = plan_ref[0, block] * tok + col
        kd = dref[...].astype(jnp.float32)
        qd = wide(qd_buf[...], tok)
        mask = (k_pos <= q_pos) & (k_pos >= wide(lo_buf[...], tok))
        mask = mask & ((kd == qd) | (qd == 0.0))
        keys = kref[:, :HD]
        vals = kref[:, HD:]
        for h in range(gsz):
            hh = g * gsz + h
            s = lax.dot_general(
                q_ref[:, hh * HD : (hh + 1) * HD],
                keys,
                (((1,), (1,)), ((), ())),
                preferred_element_type=jnp.float32,
            )
            z = jnp.where(mask, s * scale, NEG)
            top = jnp.broadcast_to(jnp.max(z, axis=1, keepdims=True), (tok, LANES))
            if not first:
                old = m_buf[hh]
                top = jnp.maximum(top, old)
                alpha = jnp.exp2(old - top)
            p = jnp.exp2(z - wide(top, tok))
            total = p[:, :LANES]
            for i in range(1, tok // LANES):
                total = total + p[:, i * LANES : (i + 1) * LANES]
            update = jnp.dot(
                p.astype(jnp.bfloat16), vals, preferred_element_type=jnp.float32
            )
            m_buf[hh] = top
            if first:
                l_buf[hh] = total
                acc_buf[hh] = update
            else:
                l_buf[hh] = l_buf[hh] * alpha + total
                acc_buf[hh] = acc_buf[hh] * alpha + update

    for g in range(kvh):
        attend(g, kv_ref.at[g], doc_ref, me, True)

    def step_body(step, carry):
        blocks = (me - 1 - step, me + 1 + step)
        arrives = (blocks[0] >= 0, blocks[1] < n)
        for g in range(kvh):
            for way in range(2):
                block = blocks[way]

                @pl.when(arrives[way])
                def _(g=g, way=way, block=block):
                    if g == 0:
                        doc_copy(way, step, dbuf.at[block], block).wait_recv()
                    kv_copy(way, step, g, kvbuf.at[block, g], block).wait_recv()

                    @pl.when(can[way])
                    def _():
                        if g == 0:
                            doc_copy(way, step + 1, dbuf.at[block], block).start()
                        kv_copy(way, step + 1, g, kvbuf.at[block, g], block).start()

            for way in range(2):
                block = blocks[way]

                @pl.when(arrives[way])
                def _(g=g, block=block):
                    attend(g, kvbuf.at[block, g], dbuf.at[block], block, False)

            @pl.when(step == n - 2)
            def _(g=g):
                finish(g)

        return carry

    def att_copy(k, g, half):
        view = att.at[d, pl.ds(half * hrows, hrows), pl.ds(g * gcols, gcols)]
        return pltpu.make_async_remote_copy(
            src_ref=view,
            dst_ref=view,
            send_sem=att_send.at[k - 1, g, half],
            recv_sem=att_recv.at[k - 1, g, half],
            device_id={"dp": lax.rem(d + k, rows)},
            device_id_type=MESH,
        )

    def finish(g):
        for half in range(halves):
            span = pl.ds(half * hrows, hrows)
            for h in range(gsz):
                hh = g * gsz + h
                total = jnp.sum(l_buf[hh, span, :], axis=1, keepdims=True)
                att[d, span, hh * HD : (hh + 1) * HD] = (
                    acc_buf[hh, span, :] / total
                ).astype(jnp.bfloat16)
            for k in range(1, rows):
                att_copy(k, g, half).start()

    lax.fori_loop(0, n - 1, step_body, 0)
    w_copy.wait()

    def part_copy(k, u):
        return pltpu.make_async_remote_copy(
            src_ref=part.at[k, u],
            dst_ref=prec.at[k, u],
            send_sem=part_send.at[k, u],
            recv_sem=part_recv.at[k, u],
            device_id={"tp": other},
            device_id_type=MESH,
        )

    home = d // per_half
    place = lax.rem(d, per_half)

    def out_view(u, spot):
        half = u // chunks
        c = u % chunks
        return out_hbm.at[
            pl.ds(half * hrows, hrows),
            pl.ds(pl.multiple_of(spot * cols + c * ccols, LANES), ccols),
        ]

    def fin_copy(k, u, spot):
        return pltpu.make_async_remote_copy(
            src_ref=fin.at[k, u],
            dst_ref=out_view(u, spot),
            send_sem=fin_send.at[k, u],
            recv_sem=fin_recv.at[spot, u],
            device_id={"dp": lax.rem(d + k, rows), "tp": home},
            device_id_type=MESH,
        )

    def loc_copy(u):
        return pltpu.make_async_copy(fin.at[0, u], out_view(u, place), loc_sem.at[u])

    def keeps(k):
        return lax.rem(lax.rem(d + k, rows), cores) == t

    def multiply(k, u):
        half = u // chunks
        c = u % chunks
        a = att[lax.rem(d + k, rows), half * hrows : (half + 1) * hrows, :]
        part[k, u] = jnp.dot(
            a,
            w_buf[:, c * ccols : (c + 1) * ccols],
            preferred_element_type=jnp.float32,
        ).astype(jnp.bfloat16)

        @pl.when(jnp.logical_not(keeps(k)))
        def _():
            part_copy(k, u).start()

    def settle(k, u):
        @pl.when(keeps(k))
        def _():
            part_copy(k, u).wait_recv()
            fin[k, u] = (
                part[k, u].astype(jnp.float32) + prec[k, u].astype(jnp.float32)
            ).astype(jnp.bfloat16)
            if k == 0:

                @pl.when(home == t)
                def _():
                    loc_copy(u).start()

                @pl.when(home != t)
                def _():
                    fin_copy(k, u, place).start()
            else:
                fin_copy(k, u, place).start()

    for k in range(rows):
        for half in range(halves):
            if k > 0:
                for g in range(kvh):
                    att_copy(k, g, half).wait_recv()
            for c in range(chunks):
                u = half * chunks + c
                multiply(k, u)
                if c > 0:
                    settle(k, u - 1)
            settle(k, half * chunks + chunks - 1)

    for spot in range(per_half):
        source = t * per_half + spot
        local = (source == d) & (lax.rem(d, cores) == t)

        @pl.when(jnp.logical_not(local))
        def _(spot=spot):
            for u in range(halves * chunks):
                fin_copy(0, u, spot).wait_recv()

        @pl.when(local)
        def _():
            for u in range(halves * chunks):
                loc_copy(u).wait()

    for k in range(rows):

        @pl.when(keeps(k))
        def _(k=k):
            for u in range(halves * chunks):
                if k == 0:

                    @pl.when(home != t)
                    def _(u=u):
                        fin_copy(k, u, place).wait_send()
                else:
                    fin_copy(k, u, place).wait_send()

        @pl.when(jnp.logical_not(keeps(k)))
        def _(k=k):
            for u in range(halves * chunks):
                part_copy(k, u).wait_send()

    for k in range(1, rows):
        for g in range(kvh):
            for half in range(halves):
                att_copy(k, g, half).wait_send()

    def drain(step, carry):
        blocks = (me - step, me + step)
        sent = ((blocks[0] >= 0) & can[0], (blocks[1] < n) & can[1])
        for way in range(2):

            @pl.when(sent[way])
            def _(way=way):
                doc_copy(way, step, dbuf.at[blocks[way]], blocks[way]).wait_send()
                for g in range(kvh):
                    kv_copy(
                        way, step, g, kvbuf.at[blocks[way], g], blocks[way]
                    ).wait_send()

        return carry

    lax.fori_loop(0, n - 1, drain, 0)


def per_device(n, rows, cores, queries, keyvals, doc_ids, plan, lengths, out_weight):
    tok = queries.shape[1]
    kvh = keyvals.shape[3] // HD
    heads = queries.shape[2] // HD
    gsz = heads // kvh
    reqs = lengths.shape[1]
    width = queries.shape[2]
    cols = out_weight.shape[1]
    halves = 2
    chunks = 4
    units = halves * chunks
    cfg = (n, rows, cores, tok, kvh, gsz, reqs, cols, halves, chunks)
    kv = (
        keyvals[0]
        .reshape(tok, 2, kvh, HD)
        .transpose(2, 0, 1, 3)
        .reshape(kvh, tok, 2 * HD)
    )
    tile = (rows, units, tok // halves, cols // chunks)
    vmem = pl.BlockSpec(memory_space=pltpu.VMEM)
    smem = pl.BlockSpec(memory_space=pltpu.SMEM)
    anym = pl.BlockSpec(memory_space=pl.ANY)
    dma = pltpu.SemaphoreType.DMA
    out = pl.pallas_call(
        functools.partial(kernel, cfg),
        out_shape=jax.ShapeDtypeStruct((tok, cols * (rows // cores)), jnp.bfloat16),
        in_specs=[smem, smem, vmem, vmem, vmem, anym],
        out_specs=anym,
        scratch_shapes=[
            pltpu.VMEM((n, kvh, tok, 2 * HD), jnp.bfloat16),
            pltpu.VMEM((n, 1, tok), jnp.int32),
            pltpu.VMEM((tok, LANES), jnp.int32),
            pltpu.VMEM((tok, LANES), jnp.float32),
            pltpu.VMEM((heads, tok, LANES), jnp.float32),
            pltpu.VMEM((heads, tok, LANES), jnp.float32),
            pltpu.VMEM((heads, tok, HD), jnp.float32),
            pltpu.VMEM((rows, tok, width), jnp.bfloat16),
            pltpu.VMEM(out_weight.shape, jnp.bfloat16),
            pltpu.VMEM(tile, jnp.bfloat16),
            pltpu.VMEM(tile, jnp.bfloat16),
            pltpu.VMEM(tile, jnp.bfloat16),
            dma,
            dma((2, n - 1, kvh)),
            dma((2, n - 1, kvh)),
            dma((2, n - 1)),
            dma((2, n - 1)),
            dma((rows - 1, kvh, halves)),
            dma((rows - 1, kvh, halves)),
            dma((rows, units)),
            dma((rows, units)),
            dma((rows, units)),
            dma((rows // cores, units)),
            dma((units,)),
        ],
        compiler_params=pltpu.CompilerParams(
            collective_id=0, has_side_effects=True, vmem_limit_bytes=60 * 1024 * 1024
        ),
        name="fused",
    )(plan, lengths, queries[0], kv, doc_ids, out_weight)
    return out[None]


def solution(mesh):
    placed = (
        P(("groups", "dp"), "ctx", "tp"),
        P(("groups", "dp"), "ctx", None, "tp"),
        P(("groups", "dp"), "ctx"),
        P(("groups", "dp"), None),
        P(("groups", "dp"), None),
        P("tp", "dp"),
    )
    sizes = mesh.shape
    return jax.shard_map(
        functools.partial(per_device, sizes["ctx"], sizes["dp"], sizes["tp"]),
        mesh=mesh,
        in_specs=placed,
        out_specs=P(("groups", "dp"), "ctx", "tp"),
        check_vma=False,
    )
```

time: 126 us -> 52.1 us (0.41)
  Pallas kernels: 0 us -> 47.4 us
  waiting for transfers between devices: 44.9 us -> 0 us
  blocking collectives: 36.8 us -> 0 us
  between operations: 13.2 us -> 0.02 us
  other arithmetic: 10.7 us -> 0 us
  matrix products: 10.2 us -> 0 us
  local copies, waits for them, and re-layouts: 7.4 us -> 4.43 us
  loops' own time: 1.51 us -> 0 us
    pallas_call x0 -> x1, Pallas kernels: none -> 47.4 us  [per_device(): pl.pallas_call(functools.partial(kernel, cfg), out_shape=jax.ShapeDtypeSt...]
    all_gather x2 -> x0, waiting for transfers between devices: 33.6 us -> none  [the longest x1 20.1 us: per_device(): lax.all_gather(attended, 'dp', axis=0, tiled=True)]
    all_to_all x1 -> x0, blocking collectives: 26.6 us -> none  [per_device(): lax.all_to_all(projected, 'dp', split_axis=0, concat_axis=1, tiled=True)]
    reduce_scatter x1 -> x0, waiting for transfers between devices: 11.3 us -> none  [per_device(): lax.psum_scatter(partials.astype(jnp.bfloat16), 'tp', scatter_dimension=1...]
    all_gather x1 -> x0, blocking collectives: 10.2 us -> none  [per_device(): doc_piece = lax.all_gather(query_doc, 'ctx', axis=0, tiled=True)]
    dot_general x5 -> x0, matrix products: 10.2 us -> none  [the longest x1 4.88 us: per_device(): jnp.dot(lax.all_gather(attended, 'dp', axis=0, tiled=True), out_weight, p...]
    reduce_sum x6 -> x0, other arithmetic: 3.03 us -> none  [the longest x2 2.04 us: attend(): new_sum = row_sum * factor + jnp.sum(probs, axis=3)]
    unnamed x6 -> x1, local copies, waits for them, and re-layouts: 4.71 us -> 2.3 us
  transfers between devices with their start and end apart: 3 -> 0, of which waited for: 3 -> 0; matrix products, arithmetic and copies ran while one was open for 5% -> 0% of each run, Pallas kernels for 0% -> 0%
where the time goes in v1:
time: 52.1 us; the launch traced here: 51.9 us
  Pallas kernels  47.4 us (91%)
  local copies, waits for them, and re-layouts  4.43 us (9%)
    pallas_call x1, Pallas kernels, per_device(): pl.pallas_call(functools.partial(kernel, cfg), out_shape=jax.ShapeDtypeSt...  47.4 us
    unnamed x1, local copies, waits for them, and re-layouts  2.3 us
    another operation x2, local copies, waits for them, and re-layouts, per_device(): kv = keyvals[0].reshape(tok, 2, kvh, HD).transpose(2, 0, 1, 3).reshape(kv...  1.26 us

profile of v1, /device:TPU:1, one launch (start us, length us, event | category | flops | bytes accessed | tf_op | source)
XLA Modules:
  0.0 51.9 jit_solution(7546667429518678465)
XLA Ops:
  0.0 1.1 %reshape_squeeze.3 = bf16[256,2,2,128]{3,2,1,0:T(2,128)(2,1)S(1)} reshape(bf16[1,256,2,256]{3,2,1,0:T(2,128)(2,1)} %param.7) | data formatting | bytes 524288 | tf_op jit(solution)/shard_map/reshape;squeeze | solution.py:384
  1.1 0.1 copy.9
  1.3 0.9 %reshape.3.kv_ref = bf16[2,256,256]{2,1,0:T(8,128)(2,1)} reshape(bf16[2,256,2,128]{3,2,1,0:T(2,128)(2,1)S(1)} %bitcast.6) | data formatting | bytes 524288 | tf_op jit(solution)/shard_map/reshape | solution.py:386
  2.1 47.4 %fused.1 = bf16[256,2048]{1,0:T(8,128)(2,1)} custom-call(s32[1,4]{1,0:T(1,128)} %plan_ref.1, s32[1,8]{1,0:T(1,128)} %len_ref.1, bf16[256,1024]{1,0:T(8,128)(2,1)} %bitcast.7, bf16[2,256,256]{2,1,0:T(8,128)(2,1)} %reshape.3.kv_ref, s32[1,256]{1,0:T(1,128)} %doc_ref.1, bf16[1024,2048]{1,0:T(8,128)(2,1)} %w_hbm.1), custom_call_target="tpu_custom_call" | custom-call | tf_op jit(solution)/shard_map/fused/pallas_call | solution.py:393
  49.6 2.3 %copy.11 = bf16[1,256,2048]{2,1,0:T(8,128)(2,1)} copy(bf16[1,256,2048]{2,1,0:T(8,128)(2,1)} %bitcast.5) | data formatting | bytes 2097152

commit v2 on v1

--- a/solution.py
+++ b/solution.py
@@ -26,7 +26,7 @@
     kv_ref,
     doc_ref,
     w_hbm,
-    out_hbm,
+    out_ref,
     kvbuf,
     dbuf,
     lo_buf,
@@ -86,15 +86,26 @@
                 device_id={"dp": lax.rem(d + k, rows), "tp": lax.rem(t + c, cores)},
                 device_id_type=MESH,
             )
+    pick_row = lax.broadcasted_iota(jnp.int32, (tok, 2 * tok), 0)
+    pick_col = lax.broadcasted_iota(jnp.int32, (tok, 2 * tok), 1)
+    for which in range(2):
+        pick = (pick_col == 2 * pick_row + which).astype(jnp.bfloat16)
+        kvbuf[me, which] = jnp.dot(
+            pick, kv_ref[...], preferred_element_type=jnp.float32
+        ).astype(jnp.bfloat16)
+
     ends = (me > 0).astype(jnp.int32) + (me < n - 1).astype(jnp.int32)
     pl.semaphore_wait(barrier, rows * cores - 1 + ends)
 
-    def kv_copy(way, step, g, src, block):
+    def lane(g):
+        return pl.ds(g * HD, HD)
+
+    def kv_copy(way, step, g, which, src, block):
         return pltpu.make_async_remote_copy(
-            src_ref=src,
-            dst_ref=kvbuf.at[block, g],
-            send_sem=kv_send.at[way, step, g],
-            recv_sem=kv_recv.at[way, step, g],
+            src_ref=src.at[which, :, lane(g)],
+            dst_ref=kvbuf.at[block, which, :, lane(g)],
+            send_sem=kv_send.at[way, step, g, which],
+            recv_sem=kv_recv.at[way, step, g, which],
             device_id={"ctx": me + 1 if way == 0 else me - 1},
             device_id_type=MESH,
         )
@@ -115,8 +126,10 @@
         @pl.when(can[way])
         def _(way=way):
             doc_copy(way, 0, doc_ref, me).start()
-            for g in range(kvh):
-                kv_copy(way, 0, g, kv_ref.at[g], me).start()
+            for which in range(2):
+                kv_copy(way, 0, 0, which, kvbuf.at[me], me).start()
+            for g in range(1, kvh):
+                kv_copy(way, 0, g, 0, kvbuf.at[me], me).start()
 
     qpos = plan_ref[0, me] * tok + lax.broadcasted_iota(jnp.int32, (tok, LANES), 0)
     low = jnp.zeros((tok, LANES), jnp.int32)
@@ -138,8 +151,8 @@
         qd = wide(qd_buf[...], tok)
         mask = (k_pos <= q_pos) & (k_pos >= wide(lo_buf[...], tok))
         mask = mask & ((kd == qd) | (qd == 0.0))
-        keys = kref[:, :HD]
-        vals = kref[:, HD:]
+        keys = kref[0, :, g * HD : (g + 1) * HD]
+        vals = kref[1, :, g * HD : (g + 1) * HD]
         for h in range(gsz):
             hh = g * gsz + h
             s = lax.dot_general(
@@ -169,40 +182,35 @@
                 l_buf[hh] = l_buf[hh] * alpha + total
                 acc_buf[hh] = acc_buf[hh] * alpha + update
 
-    for g in range(kvh):
-        attend(g, kv_ref.at[g], doc_ref, me, True)
-
-    def step_body(step, carry):
+    def receive(g, step):
         blocks = (me - 1 - step, me + 1 + step)
         arrives = (blocks[0] >= 0, blocks[1] < n)
-        for g in range(kvh):
-            for way in range(2):
-                block = blocks[way]
-
-                @pl.when(arrives[way])
-                def _(g=g, way=way, block=block):
+        for way in range(2):
+            block = blocks[way]
+
+            @pl.when(arrives[way])
+            def _(way=way, block=block):
+                if g == 0:
+                    doc_copy(way, step, dbuf.at[block], block).wait_recv()
+                for which in range(2):
+                    kv_copy(way, step, g, which, kvbuf.at[block], block).wait_recv()
+
+                @pl.when(can[way])
+                def _():
                     if g == 0:
-                        doc_copy(way, step, dbuf.at[block], block).wait_recv()
-                    kv_copy(way, step, g, kvbuf.at[block, g], block).wait_recv()
-
-                    @pl.when(can[way])
-                    def _():
-                        if g == 0:
-                            doc_copy(way, step + 1, dbuf.at[block], block).start()
-                        kv_copy(way, step + 1, g, kvbuf.at[block, g], block).start()
-
-            for way in range(2):
-                block = blocks[way]
-
-                @pl.when(arrives[way])
-                def _(g=g, block=block):
-                    attend(g, kvbuf.at[block, g], dbuf.at[block], block, False)
-
-            @pl.when(step == n - 2)
-            def _(g=g):
-                finish(g)
-
-        return carry
+                        doc_copy(way, step + 1, dbuf.at[block], block).start()
+                    for which in range(2):
+                        kv_copy(way, step + 1, g, which, kvbuf.at[block], block).start()
+
+    def absorb(g, step):
+        blocks = (me - 1 - step, me + 1 + step)
+        arrives = (blocks[0] >= 0, blocks[1] < n)
+        for way in range(2):
+            block = blocks[way]
+
+            @pl.when(arrives[way])
+            def _(block=block):
+                attend(g, kvbuf.at[block], dbuf.at[block], block, False)
 
     def att_copy(k, g, half):
         view = att.at[d, pl.ds(half * hrows, hrows), pl.ds(g * gcols, gcols)]
@@ -227,7 +235,42 @@
             for k in range(1, rows):
                 att_copy(k, g, half).start()
 
-    lax.fori_loop(0, n - 1, step_body, 0)
+    for g in range(kvh):
+        attend(g, kvbuf.at[me], doc_ref, me, True)
+
+    def step_body(step, carry):
+        @pl.when(step < n - 1)
+        def _():
+            receive(0, step)
+
+        @pl.when(step == 0)
+        def _():
+            for way in range(2):
+
+                @pl.when(can[way])
+                def _(way=way):
+                    for g in range(1, kvh):
+                        kv_copy(way, 0, g, 1, kvbuf.at[me], me).start()
+
+        @pl.when(step < n - 1)
+        def _():
+            absorb(0, step)
+
+        @pl.when(step == n - 2)
+        def _():
+            finish(0)
+
+        @pl.when(step > 0)
+        def _():
+            for g in range(1, kvh):
+                receive(g, step - 1)
+                absorb(g, step - 1)
+
+        return carry
+
+    lax.fori_loop(0, n, step_body, 0)
+    for g in range(1, kvh):
+        finish(g)
     w_copy.wait()
 
     def part_copy(k, u):
@@ -246,7 +289,7 @@
     def out_view(u, spot):
         half = u // chunks
         c = u % chunks
-        return out_hbm.at[
+        return out_ref.at[
             pl.ds(half * hrows, hrows),
             pl.ds(pl.multiple_of(spot * cols + c * ccols, LANES), ccols),
         ]
@@ -358,9 +401,10 @@
             def _(way=way):
                 doc_copy(way, step, dbuf.at[blocks[way]], blocks[way]).wait_send()
                 for g in range(kvh):
-                    kv_copy(
-                        way, step, g, kvbuf.at[blocks[way], g], blocks[way]
-                    ).wait_send()
+                    for which in range(2):
+                        kv_copy(
+                            way, step, g, which, kvbuf.at[blocks[way]], blocks[way]
+                        ).wait_send()
 
         return carry
 
@@ -379,24 +423,19 @@
     chunks = 4
     units = halves * chunks
     cfg = (n, rows, cores, tok, kvh, gsz, reqs, cols, halves, chunks)
-    kv = (
-        keyvals[0]
-        .reshape(tok, 2, kvh, HD)
-        .transpose(2, 0, 1, 3)
-        .reshape(kvh, tok, 2 * HD)
-    )
+    kv = keyvals[0].reshape(2 * tok, kvh * HD)
     tile = (rows, units, tok // halves, cols // chunks)
     vmem = pl.BlockSpec(memory_space=pltpu.VMEM)
     smem = pl.BlockSpec(memory_space=pltpu.SMEM)
-    anym = pl.BlockSpec(memory_space=pl.ANY)
+    hbm = pl.BlockSpec(memory_space=pltpu.HBM)
     dma = pltpu.SemaphoreType.DMA
     out = pl.pallas_call(
         functools.partial(kernel, cfg),
         out_shape=jax.ShapeDtypeStruct((tok, cols * (rows // cores)), jnp.bfloat16),
-        in_specs=[smem, smem, vmem, vmem, vmem, anym],
-        out_specs=anym,
+        in_specs=[smem, smem, vmem, vmem, vmem, hbm],
+        out_specs=vmem,
         scratch_shapes=[
-            pltpu.VMEM((n, kvh, tok, 2 * HD), jnp.bfloat16),
+            pltpu.VMEM((n, 2, tok, kvh * HD), jnp.bfloat16),
             pltpu.VMEM((n, 1, tok), jnp.int32),
             pltpu.VMEM((tok, LANES), jnp.int32),
             pltpu.VMEM((tok, LANES), jnp.float32),
@@ -409,8 +448,8 @@
             pltpu.VMEM(tile, jnp.bfloat16),
             pltpu.VMEM(tile, jnp.bfloat16),
             dma,
-            dma((2, n - 1, kvh)),
-            dma((2, n - 1, kvh)),
+            dma((2, n - 1, kvh, 2)),
+            dma((2, n - 1, kvh, 2)),
             dma((2, n - 1)),
             dma((2, n - 1)),
             dma((rows - 1, kvh, halves)),
@@ -422,7 +461,7 @@
             dma((units,)),
         ],
         compiler_params=pltpu.CompilerParams(
-            collective_id=0, has_side_effects=True, vmem_limit_bytes=60 * 1024 * 1024
+            collective_id=0, has_side_effects=True, vmem_limit_bytes=61 * 1024 * 1024
         ),
         name="fused",
     )(plan, lengths, queries[0], kv, doc_ids, out_weight)

time: 52.1 us -> 51.4 us (0.987)
    reshape x1 -> x0, local copies, waits for them, and re-layouts: 0.87 us -> none  [per_device(): kv = keyvals[0].reshape(tok, 2, kvh, HD).transpose(2, 0, 1, 3).reshape(kv...]
    another operation x2 -> x1, local copies, waits for them, and re-layouts: 1.26 us -> 1.75 us  [per_device(): kv = keyvals[0].reshape(2 * tok, kvh * HD)]
where the time goes in v2:
time: 51.4 us; the launch traced here: 51.2 us
  Pallas kernels  47.1 us (92%)
  local copies, waits for them, and re-layouts  4.06 us (8%)
    pallas_call x1, Pallas kernels, per_device(): pl.pallas_call(functools.partial(kernel, cfg), out_shape=jax.ShapeDtypeSt...  47.1 us
    unnamed x1, local copies, waits for them, and re-layouts  2.3 us
    another operation x1, local copies, waits for them, and re-layouts, per_device(): kv = keyvals[0].reshape(2 * tok, kvh * HD)  1.75 us

profile of v2, /device:TPU:1, one launch (start us, length us, event | category | flops | bytes accessed | tf_op | source)
XLA Modules:
  0.0 51.2 jit_solution(12632836940167134836)
XLA Ops:
  0.0 1.8 %reshape_squeeze.3.kv_ref = bf16[512,256]{1,0:T(8,128)(2,1)} reshape(bf16[1,256,2,256]{3,2,1,0:T(2,128)(2,1)} %param.7) | data formatting | bytes 524288 | tf_op jit(solution)/shard_map/reshape;squeeze | solution.py:426
  1.8 47.1 %fused.1 = bf16[256,2048]{1,0:T(8,128)(2,1)} custom-call(s32[1,4]{1,0:T(1,128)} %plan_ref.1, s32[1,8]{1,0:T(1,128)} %len_ref.1, bf16[256,1024]{1,0:T(8,128)(2,1)} %bitcast.3, bf16[512,256]{1,0:T(8,128)(2,1)} %reshape_squeeze.3.kv_ref, s32[1,256]{1,0:T(1,128)} %doc_ref.1, bf16[1024,2048]{1,0:T(8,128)(2,1)} %w_hbm.1), custom_call_target="tpu_custom_call" | custom-call | tf_op jit(solution)/shard_map/fused/pallas_call | solution.py:432
  48.9 2.3 %copy.8 = bf16[1,256,2048]{2,1,0:T(8,128)(2,1)} copy(bf16[1,256,2048]{2,1,0:T(8,128)(2,1)} %bitcast.2) | data formatting | bytes 2097152

commit v3 on v2

--- a/solution.py
+++ b/solution.py
@@ -39,6 +39,10 @@
     part,
     prec,
     fin,
+    far_w,
+    far_part,
+    far_prec,
+    far_fin,
     w_sem,
     kv_send,
     kv_recv,
@@ -51,11 +55,20 @@
     fin_send,
     fin_recv,
     loc_sem,
+    far_send,
+    far_recv,
+    swap_send,
+    swap_recv,
+    fp_send,
+    fp_recv,
+    far_loc,
 ):
-    n, rows, cores, tok, kvh, gsz, reqs, cols, halves, chunks = cfg
+    n, rows, cores, packs, tok, kvh, gsz, reqs, cols, halves, chunks = cfg
     me = lax.axis_index("ctx")
     d = lax.axis_index("dp")
     t = lax.axis_index("tp")
+    gy = lax.axis_index("groups")
+    kept = chunks - packs
     other = 1 - t
     hrows = tok // halves
     ccols = cols // chunks
@@ -86,6 +99,13 @@
                 device_id={"dp": lax.rem(d + k, rows), "tp": lax.rem(t + c, cores)},
                 device_id_type=MESH,
             )
+    for j in range(1, packs):
+        pl.semaphore_signal(
+            barrier,
+            inc=1,
+            device_id={"groups": lax.rem(gy + j, packs)},
+            device_id_type=MESH,
+        )
     pick_row = lax.broadcasted_iota(jnp.int32, (tok, 2 * tok), 0)
     pick_col = lax.broadcasted_iota(jnp.int32, (tok, 2 * tok), 1)
     for which in range(2):
@@ -95,7 +115,7 @@
         ).astype(jnp.bfloat16)
 
     ends = (me > 0).astype(jnp.int32) + (me < n - 1).astype(jnp.int32)
-    pl.semaphore_wait(barrier, rows * cores - 1 + ends)
+    pl.semaphore_wait(barrier, rows * cores - 1 + packs - 1 + ends)
 
     def lane(g):
         return pl.ds(g * HD, HD)
@@ -130,6 +150,30 @@
                 kv_copy(way, 0, 0, which, kvbuf.at[me], me).start()
             for g in range(1, kvh):
                 kv_copy(way, 0, g, 0, kvbuf.at[me], me).start()
+
+    def far_copy(k):
+        start = pl.multiple_of((kept + gy) * ccols, LANES)
+        return pltpu.make_async_remote_copy(
+            src_ref=w_hbm.at[:, pl.ds(start, ccols)],
+            dst_ref=far_w.at[k - 1, gy],
+            send_sem=far_send.at[k - 1],
+            recv_sem=far_recv.at[k - 1],
+            device_id={"dp": lax.rem(d + k, rows)},
+            device_id_type=MESH,
+        )
+
+    def swap_copy(k, j, pack):
+        return pltpu.make_async_remote_copy(
+            src_ref=far_w.at[k - 1, pack],
+            dst_ref=far_w.at[k - 1, pack],
+            send_sem=swap_send.at[k - 1, j - 1],
+            recv_sem=swap_recv.at[k - 1, j - 1],
+            device_id={"groups": lax.rem(gy + j, packs)},
+            device_id_type=MESH,
+        )
+
+    for k in range(1, rows):
+        far_copy(k).start()
 
     qpos = plan_ref[0, me] * tok + lax.broadcasted_iota(jnp.int32, (tok, LANES), 0)
     low = jnp.zeros((tok, LANES), jnp.int32)
@@ -343,49 +387,141 @@
             else:
                 fin_copy(k, u, place).start()
 
+    def far_home(k):
+        source = lax.rem(d - k + rows, rows)
+        return source // per_half, lax.rem(source, per_half)
+
+    def far_pack(j):
+        return lax.rem(gy - j + packs, packs)
+
+    def far_pcopy(k, j, half):
+        return pltpu.make_async_remote_copy(
+            src_ref=far_part.at[k - 1, j, half],
+            dst_ref=far_prec.at[k - 1, j, half],
+            send_sem=fp_send.at[k - 1, j, half],
+            recv_sem=fp_recv.at[k - 1, j, half],
+            device_id={"tp": other},
+            device_id_type=MESH,
+        )
+
+    def far_lcopy(k, j, half):
+        column = far_home(k)[1] * cols + (kept + far_pack(j)) * ccols
+        return pltpu.make_async_copy(
+            far_fin.at[k - 1, j, half],
+            out_ref.at[
+                pl.ds(half * hrows, hrows), pl.ds(pl.multiple_of(column, LANES), ccols)
+            ],
+            far_loc.at[k - 1, j, half],
+        )
+
+    def far_multiply(k, j):
+        for half in range(halves):
+            far_part[k - 1, j, half] = jnp.dot(
+                att[d, half * hrows : (half + 1) * hrows, :],
+                far_w[k - 1, far_pack(j)],
+                preferred_element_type=jnp.float32,
+            ).astype(jnp.bfloat16)
+
+            @pl.when(far_home(k)[0] != t)
+            def _(half=half):
+                far_pcopy(k, j, half).start()
+
+    def far_settle(k, j):
+        @pl.when(far_home(k)[0] == t)
+        def _():
+            for half in range(halves):
+                far_pcopy(k, j, half).wait_recv()
+                far_fin[k - 1, j, half] = (
+                    far_part[k - 1, j, half].astype(jnp.float32)
+                    + far_prec[k - 1, j, half].astype(jnp.float32)
+                ).astype(jnp.bfloat16)
+                far_lcopy(k, j, half).start()
+
+    for k in range(1, rows):
+        far_copy(k).wait_recv()
+        for j in range(1, packs):
+            swap_copy(k, j, gy).start()
+
     for k in range(rows):
+        limit = chunks if k == 0 else kept
         for half in range(halves):
             if k > 0:
                 for g in range(kvh):
                     att_copy(k, g, half).wait_recv()
-            for c in range(chunks):
+            for c in range(limit):
                 u = half * chunks + c
                 multiply(k, u)
                 if c > 0:
                     settle(k, u - 1)
-            settle(k, half * chunks + chunks - 1)
-
+            settle(k, half * chunks + limit - 1)
+        if k == 0:
+            for kk in range(1, rows):
+                far_multiply(kk, 0)
+
+    for k in range(1, rows):
+        for j in range(1, packs):
+            swap_copy(k, j, far_pack(j)).wait_recv()
+            far_multiply(k, j)
+        for j in range(packs):
+            far_settle(k, j)
+
+    own_units = [h * chunks + c for h in range(halves) for c in range(chunks)]
+    row_units = [h * chunks + c for h in range(halves) for c in range(kept)]
     for spot in range(per_half):
         source = t * per_half + spot
-        local = (source == d) & (lax.rem(d, cores) == t)
-
-        @pl.when(jnp.logical_not(local))
+        near = source == d
+        local = near & (lax.rem(d, cores) == t)
+
+        @pl.when(jnp.logical_not(near))
         def _(spot=spot):
-            for u in range(halves * chunks):
+            for u in row_units:
                 fin_copy(0, u, spot).wait_recv()
 
+        @pl.when(near & jnp.logical_not(local))
+        def _(spot=spot):
+            for u in own_units:
+                fin_copy(0, u, spot).wait_recv()
+
         @pl.when(local)
         def _():
-            for u in range(halves * chunks):
+            for u in own_units:
                 loc_copy(u).wait()
 
     for k in range(rows):
 
         @pl.when(keeps(k))
         def _(k=k):
-            for u in range(halves * chunks):
-                if k == 0:
-
-                    @pl.when(home != t)
-                    def _(u=u):
+            if k == 0:
+
+                @pl.when(home != t)
+                def _():
+                    for u in own_units:
                         fin_copy(k, u, place).wait_send()
-                else:
+            else:
+                for u in row_units:
                     fin_copy(k, u, place).wait_send()
 
         @pl.when(jnp.logical_not(keeps(k)))
         def _(k=k):
-            for u in range(halves * chunks):
+            for u in own_units if k == 0 else row_units:
                 part_copy(k, u).wait_send()
+
+    for k in range(1, rows):
+        far_copy(k).wait_send()
+        for j in range(1, packs):
+            swap_copy(k, j, gy).wait_send()
+
+        @pl.when(far_home(k)[0] == t)
+        def _(k=k):
+            for j in range(packs):
+                for half in range(halves):
+                    far_lcopy(k, j, half).wait()
+
+        @pl.when(far_home(k)[0] != t)
+        def _(k=k):
+            for j in range(packs):
+                for half in range(halves):
+                    far_pcopy(k, j, half).wait_send()
 
     for k in range(1, rows):
         for g in range(kvh):
@@ -411,7 +547,7 @@
     lax.fori_loop(0, n - 1, drain, 0)
 
 
-def per_device(n, rows, cores, queries, keyvals, doc_ids, plan, lengths, out_weight):
+def per_device(n, rows, cores, packs, queries, keyvals, doc_ids, plan, lengths, out_weight):
     tok = queries.shape[1]
     kvh = keyvals.shape[3] // HD
     heads = queries.shape[2] // HD
@@ -420,11 +556,12 @@
     width = queries.shape[2]
     cols = out_weight.shape[1]
     halves = 2
-    chunks = 4
+    chunks = cols // (2 * LANES)
     units = halves * chunks
-    cfg = (n, rows, cores, tok, kvh, gsz, reqs, cols, halves, chunks)
+    cfg = (n, rows, cores, packs, tok, kvh, gsz, reqs, cols, halves, chunks)
     kv = keyvals[0].reshape(2 * tok, kvh * HD)
     tile = (rows, units, tok // halves, cols // chunks)
+    far = (rows - 1, packs, halves, tok // halves, cols // chunks)
     vmem = pl.BlockSpec(memory_space=pltpu.VMEM)
     smem = pl.BlockSpec(memory_space=pltpu.SMEM)
     hbm = pl.BlockSpec(memory_space=pltpu.HBM)
@@ -433,7 +570,7 @@
         functools.partial(kernel, cfg),
         out_shape=jax.ShapeDtypeStruct((tok, cols * (rows // cores)), jnp.bfloat16),
         in_specs=[smem, smem, vmem, vmem, vmem, hbm],
-        out_specs=vmem,
+        out_specs=hbm,
         scratch_shapes=[
             pltpu.VMEM((n, 2, tok, kvh * HD), jnp.bfloat16),
             pltpu.VMEM((n, 1, tok), jnp.int32),
@@ -447,6 +584,10 @@
             pltpu.VMEM(tile, jnp.bfloat16),
             pltpu.VMEM(tile, jnp.bfloat16),
             pltpu.VMEM(tile, jnp.bfloat16),
+            pltpu.VMEM((rows - 1, packs, width, cols // chunks), jnp.bfloat16),
+            pltpu.VMEM(far, jnp.bfloat16),
+            pltpu.VMEM(far, jnp.bfloat16),
+            pltpu.VMEM(far, jnp.bfloat16),
             dma,
             dma((2, n - 1, kvh, 2)),
             dma((2, n - 1, kvh, 2)),
@@ -459,6 +600,13 @@
             dma((rows, units)),
             dma((rows // cores, units)),
             dma((units,)),
+            dma((rows - 1,)),
+            dma((rows - 1,)),
+            dma((rows - 1, packs - 1)),
+            dma((rows - 1, packs - 1)),
+            dma((rows - 1, packs, halves)),
+            dma((rows - 1, packs, halves)),
+            dma((rows - 1, packs, halves)),
         ],
         compiler_params=pltpu.CompilerParams(
             collective_id=0, has_side_effects=True, vmem_limit_bytes=61 * 1024 * 1024
@@ -479,7 +627,7 @@
     )
     sizes = mesh.shape
     return jax.shard_map(
-        functools.partial(per_device, sizes["ctx"], sizes["dp"], sizes["tp"]),
+        functools.partial(per_device, sizes["ctx"], sizes["dp"], sizes["tp"], sizes["groups"]),
         mesh=mesh,
         in_specs=placed,
         out_specs=P(("groups", "dp"), "ctx", "tp"),

time: 51.4 us -> 49.5 us (0.963)
  Pallas kernels: 47.1 us -> 45.3 us
    pallas_call x1, Pallas kernels: 47.1 us -> 45.3 us  [per_device(): pl.pallas_call(functools.partial(kernel, cfg), out_shape=jax.ShapeDtypeSt...]
where the time goes in v3:
time: 49.5 us; the launch traced here: 49.3 us
  Pallas kernels  45.3 us (92%)
  local copies, waits for them, and re-layouts  4.06 us (8%)
    pallas_call x1, Pallas kernels, per_device(): pl.pallas_call(functools.partial(kernel, cfg), out_shape=jax.ShapeDtypeSt...  45.3 us
    unnamed x1, local copies, waits for them, and re-layouts  2.3 us
    another operation x1, local copies, waits for them, and re-layouts, per_device(): kv = keyvals[0].reshape(2 * tok, kvh * HD)  1.75 us

profile of v3, /device:TPU:1, one launch (start us, length us, event | category | flops | bytes accessed | tf_op | source)
XLA Modules:
  0.0 49.3 jit_solution(3414156819801698773)
XLA Ops:
  0.0 1.8 %reshape_squeeze.3.kv_ref = bf16[512,256]{1,0:T(8,128)(2,1)} reshape(bf16[1,256,2,256]{3,2,1,0:T(2,128)(2,1)} %param.7) | data formatting | bytes 524288 | tf_op jit(solution)/shard_map/reshape;squeeze | solution.py:562
  1.8 45.3 %fused.1 = bf16[256,2048]{1,0:T(8,128)(2,1)} custom-call(s32[1,4]{1,0:T(1,128)} %plan_ref.1, s32[1,8]{1,0:T(1,128)} %len_ref.1, bf16[256,1024]{1,0:T(8,128)(2,1)} %bitcast.3, bf16[512,256]{1,0:T(8,128)(2,1)} %reshape_squeeze.3.kv_ref, s32[1,256]{1,0:T(1,128)} %doc_ref.1, bf16[1024,2048]{1,0:T(8,128)(2,1)} %w_hbm.1), custom_call_target="tpu_custom_call" | custom-call | tf_op jit(solution)/shard_map/fused/pallas_call | solution.py:569
  47.0 2.3 %copy.8 = bf16[1,256,2048]{2,1,0:T(8,128)(2,1)} copy(bf16[1,256,2048]{2,1,0:T(8,128)(2,1)} %bitcast.2) | data formatting | bytes 2097152
